TPU v7x, 32 devices: a whole 2x2x4 slice. The times are simulated.
32 devices in a mesh: pipe: 4 (over x, core), dp: 2 (over y), tensor: 4 (over z).
Axes of the slice: x: 2, y: 2, z: 4, core: 2. Of those that a mesh axis runs over, the one named last changes fastest.
Arguments:
- grad_top: bfloat16 [2, 128, 12288], P(None, None, ('dp', 'tensor')), may hold values from -1.1953125 to 1.1953125
- inputs: bfloat16 [4, 2, 128, 12288], P('pipe', None, None, ('dp', 'tensor')), may hold values from -6 to 6
- pre: bfloat16 [4, 2, 128, 6144], P('pipe', None, 'dp', 'tensor'), may hold values from -6 to 6
- weight_in: bfloat16 [4, 6144, 12288], P('pipe', 'tensor', 'dp'), may hold values from -0.0546875 to 0.0546875
- weight_out: bfloat16 [4, 6144, 12288], P('pipe', 'tensor', 'dp'), may hold values from -0.0546875 to 0.0546875
Outputs:
- weight_in_grad: bfloat16 [4, 6144, 12288], P('pipe', 'tensor', 'dp')
- weight_out_grad: bfloat16 [4, 6144, 12288], P('pipe', 'tensor', 'dp')
- section_grads: bfloat16 [4, 2, 128, 12288], P('pipe', None, None, ('dp', 'tensor'))
All inputs are finite; a program needn't handle non-finite values.
Results may differ from a plain program's by a relative error of at most 0.024.
Values may be sent and summed in bfloat16 or wider, within the bound.
A program may use at most 512 MiB of HBM per device.

v0:
```python
import math
import jax
import jax.numpy as jnp
from jax import lax
from jax.sharding import PartitionSpec as P


def shifted(block, axis, distance):
    devices = range(lax.axis_size(axis))
    route = [(i - distance, i) for i in devices if i - distance in devices]
    return lax.ppermute(block, axis, route)


def gelu_pair(values):
    root_coef = math.sqrt(2.0 / math.pi)
    inner = root_coef * (values + 0.044715 * values * values * values)
    tangent = jnp.tanh(inner)
    activ = 0.5 * values * (1.0 + tangent)
    slope = 0.5 * (1.0 + tangent) + 0.5 * values * (1.0 - tangent * tangent) * root_coef * (
        1.0 + 3.0 * 0.044715 * values * values
    )
    return (activ, slope)


def on_device(grad_top, inputs, pre, weight_in, weight_out):
    sections = lax.axis_size("pipe")
    section = lax.axis_index("pipe")
    micro = grad_top.shape[0]
    local_in = weight_in[0]
    local_out = weight_out[0]
    contract = (((0,), (0,)), ((), ()))
    accum_in = jnp.zeros(local_in.shape, jnp.float32)
    accum_out = jnp.zeros(local_out.shape, jnp.float32)
    grads_out = jnp.zeros(grad_top.shape, jnp.bfloat16)
    outgoing = grad_top[0]
    for timestep in range(micro + sections - 1):
        micro_index = timestep - (sections - 1 - section)
        valid = jnp.logical_and(micro_index >= 0, micro_index < micro)
        clipped = jnp.clip(micro_index, 0, micro - 1)
        top_grad = lax.dynamic_index_in_dim(grad_top, clipped, 0, False)
        if timestep == 0:
            current = top_grad
        else:
            received = shifted(outgoing, "pipe", -1)
            current = jnp.where(section == sections - 1, top_grad, received)
        layer_input = lax.dynamic_index_in_dim(inputs[0], clipped, 0, False)
        pre_local = lax.dynamic_index_in_dim(pre[0], clipped, 0, False)
        grad_cols, input_cols = (
            lax.all_gather(current, "tensor", axis=1, tiled=True),
            lax.all_gather(layer_input, "tensor", axis=1, tiled=True),
        )
        head_part = lax.dot_general(
            grad_cols, local_out, (((1,), (1,)), ((), ())), preferred_element_type=jnp.float32
        )
        head_grad = lax.psum(head_part.astype(jnp.bfloat16), "dp").astype(jnp.float32)
        pre_all = lax.all_gather(pre_local, "dp", axis=0, tiled=True)
        activ, slope = gelu_pair(pre_all.astype(jnp.float32))
        head_delta = (head_grad * slope).astype(jnp.bfloat16)
        activated = activ.astype(jnp.bfloat16)
        partial_value = jnp.dot(head_delta, local_in, preferred_element_type=jnp.float32)
        summed = lax.psum_scatter(
            partial_value.astype(jnp.bfloat16), "tensor", scatter_dimension=1, tiled=True
        ).astype(jnp.float32)
        new_grad = (current.astype(jnp.float32) + summed).astype(jnp.bfloat16)
        out_term = lax.dot_general(
            activated, grad_cols, contract, preferred_element_type=jnp.float32
        )
        in_term = lax.dot_general(
            head_delta, input_cols, contract, preferred_element_type=jnp.float32
        )
        accum_out = accum_out + jnp.where(valid, out_term, 0.0)
        accum_in = accum_in + jnp.where(valid, in_term, 0.0)
        previous = lax.dynamic_index_in_dim(grads_out, clipped, 0, False)
        grads_out = lax.dynamic_update_index_in_dim(
            grads_out, jnp.where(valid, new_grad, previous), clipped, 0
        )
        outgoing = new_grad
    return (
        accum_in.astype(jnp.bfloat16)[None],
        accum_out.astype(jnp.bfloat16)[None],
        grads_out[None],
    )


def solution(mesh):
    placed = (
        P(None, None, ("dp", "tensor")),
        P("pipe", None, None, ("dp", "tensor")),
        P("pipe", None, "dp", "tensor"),
        P("pipe", "tensor", "dp"),
        P("pipe", "tensor", "dp"),
    )
    return jax.shard_map(
        on_device,
        mesh=mesh,
        in_specs=placed,
        out_specs=(
            P("pipe", "tensor", "dp"),
            P("pipe", "tensor", "dp"),
            P("pipe", None, None, ("dp", "tensor")),
        ),
        check_vma=False,
    )
```

profile of v0, /device:TPU:0, one launch (start us, length us, event | category | flops | bytes accessed | tf_op | source)
XLA Modules:
  0.0 836.4 jit_solution(14600435980791823250)
XLA Ops:
  7.2 1.8 constant_dynamic-slice_fusion.13
  9.1 40.8 %all-gather.30.cloned.1.call-done = bf16[1,128,6144]{2,1,0:T(8,128)(2,1)} async-done(((bf16[1,128,1536]{2,1,0:T(8,128)(2,1)}), bf16[1,128,6144]{2,1,0:T(8,128)(2,1)}) %all-gather.30.cloned.1.call-update) | async-done | bytes 1572880 | tf_op jit(solution)/shard_map/all_gather | solution.py:49
  49.9 14.0 %fusion.37 = bf16[128,1536]{1,0:T(8,128)(2,1)} fusion(bf16[1,1536,6144]{2,1,0:T(8,128)(2,1)} %param.9, bf16[1,128,6144]{2,1,0:T(8,128)(2,1)} %all-gather.30.cloned.1.call-done), kind=kOutput, calls=%fused_computation.29 | convolution fusion | flops 2416115712 | bytes 20840448 | tf_op jit(solution)/shard_map/dot_general | solution.py:52
  64.0 0.8 constant_dynamic-slice_fusion.4
  64.8 9.4 %all-gather.1 = bf16[1,1,128,1536]{3,2,1,0:T(8,128)(2,1)S(1)} all-gather(bf16[1,1,64,1536]{3,2,1,0:T(8,128)(2,1)S(1)} %get-tuple-element.19), channel_id=3, replica_groups=mesh['pipe'=4,'dp'=2,'tensor'=4] {'dp'}, dimensions={2}, use_global_device_ids=true | all-gather | bytes 589824 | tf_op jit(solution)/shard_map/all_gather | solution.py:56
  74.2 15.2 %all-reduce.6.cloned.1.call-done = bf16[128,1536]{1,0:T(8,128)(2,1)} async-done(((bf16[128,1536]{1,0:T(8,128)(2,1)}), bf16[128,1536]{1,0:T(8,128)(2,1)}) %all-reduce.6.cloned.1.call-update) | async-done | bytes 393232 | tf_op jit(solution)/shard_map/psum | solution.py:55
  89.5 10.7 %fusion.22 = bf16[128,6144]{1,0:T(8,128)(2,1)} fusion(bf16[1,1536,6144]{2,1,0:T(8,128)(2,1)} %param.8, bf16[128,1536]{1,0:T(8,128)(2,1)} %all-reduce.6.cloned.1.call-done, bf16[1,1,128,1536]{3,2,1,0:T(8,128)(2,1)S(1)} %all-gather.1), kind=kOutput, calls=%fused_computation.24 | convolution fusion | flops 2420834304 | bytes 21233664 | tf_op jit(solution)/shard_map/dot_general | solution.py:60
  100.2 35.5 %reduce-scatter.6.cloned.1.call-done = bf16[128,1536]{1,0:T(8,128)(2,1)} async-done(((bf16[128,6144]{1,0:T(8,128)(2,1)}), bf16[128,1536]{1,0:T(8,128)(2,1)}) %reduce-scatter.6.cloned.1.call-update) | async-done | bytes 393232 | tf_op jit(solution)/shard_map/reduce_scatter | solution.py:61
  135.8 1.1 bitcast_dynamic-update-slice_fusion.3
  137.0 1.3 collective-permute-start
  138.3 2.3 collective-permute-done
  140.6 0.8 bitcast_select_fusion.6
  141.7 39.8 %all-gather.22.cloned.1.call-done = bf16[128,6144]{1,0:T(8,128)(2,1)} async-done(((bf16[128,1536]{1,0:T(8,128)(2,1)}), bf16[128,6144]{1,0:T(8,128)(2,1)}) %all-gather.22.cloned.1.call-update) | async-done | bytes 1572880 | tf_op jit(solution)/shard_map/all_gather | solution.py:49
  181.5 14.0 %fusion.40 = bf16[128,1536]{1,0:T(8,128)(2,1)} fusion(bf16[128,6144]{1,0:T(8,128)(2,1)} %all-gather.22.cloned.1.call-done, bf16[1,1536,6144]{2,1,0:T(8,128)(2,1)} %param.9), kind=kOutput, calls=%fused_computation.30 | convolution fusion | flops 2416115712 | bytes 20840448 | tf_op jit(solution)/shard_map/dot_general | solution.py:52
  195.6 8.2 all-gather.3
  203.8 16.6 %all-reduce.8.cloned.1.call-done = bf16[128,1536]{1,0:T(8,128)(2,1)} async-done(((bf16[128,1536]{1,0:T(8,128)(2,1)}), bf16[128,1536]{1,0:T(8,128)(2,1)}) %all-reduce.8.cloned.1.call-update) | async-done | bytes 393232 | tf_op jit(solution)/shard_map/psum | solution.py:55
  220.4 10.7 %fusion.25 = bf16[128,6144]{1,0:T(8,128)(2,1)} fusion(bf16[1,1536,6144]{2,1,0:T(8,128)(2,1)} %param.8, bf16[128,1536]{1,0:T(8,128)(2,1)} %all-reduce.8.cloned.1.call-done, bf16[1,1,128,1536]{3,2,1,0:T(8,128)(2,1)S(1)} %all-gather.3), kind=kOutput, calls=%fused_computation.25 | convolution fusion | flops 2420834304 | bytes 21233664 | tf_op jit(solution)/shard_map/dot_general | solution.py:60
  231.2 35.5 %reduce-scatter.8.cloned.1.call-done = bf16[128,1536]{1,0:T(8,128)(2,1)} async-done(((bf16[128,6144]{1,0:T(8,128)(2,1)}), bf16[128,1536]{1,0:T(8,128)(2,1)}) %reduce-scatter.8.cloned.1.call-update) | async-done | bytes 393232 | tf_op jit(solution)/shard_map/reduce_scatter | solution.py:61
  266.7 1.2 bitcast_dynamic-update-slice_fusion.2
  267.9 1.3 collective-permute-start.1
  269.2 2.3 collective-permute-done.1
  272.9 39.5 %all-gather.24.cloned.1.call-done = bf16[128,6144]{1,0:T(8,128)(2,1)} async-done(((bf16[128,1536]{1,0:T(8,128)(2,1)}), bf16[128,6144]{1,0:T(8,128)(2,1)}) %all-gather.24.cloned.1.call-update) | async-done | bytes 1572880 | tf_op jit(solution)/shard_map/all_gather | solution.py:49
  312.4 14.0 %fusion.43 = bf16[128,1536]{1,0:T(8,128)(2,1)} fusion(bf16[128,6144]{1,0:T(8,128)(2,1)} %all-gather.24.cloned.1.call-done, bf16[1,1536,6144]{2,1,0:T(8,128)(2,1)} %param.9), kind=kOutput, calls=%fused_computation.31 | convolution fusion | flops 2416115712 | bytes 20840448 | tf_op jit(solution)/shard_map/dot_general | solution.py:52
  326.5 8.3 all-gather.5
  334.7 16.6 %all-reduce.10.cloned.1.call-done = bf16[128,1536]{1,0:T(8,128)(2,1)} async-done(((bf16[128,1536]{1,0:T(8,128)(2,1)}), bf16[128,1536]{1,0:T(8,128)(2,1)}) %all-reduce.10.cloned.1.call-update) | async-done | bytes 393232 | tf_op jit(solution)/shard_map/psum | solution.py:55
  351.3 10.7 %fusion.28 = bf16[128,6144]{1,0:T(8,128)(2,1)} fusion(bf16[1,1536,6144]{2,1,0:T(8,128)(2,1)} %param.8, bf16[128,1536]{1,0:T(8,128)(2,1)} %all-reduce.10.cloned.1.call-done, bf16[1,1,128,1536]{3,2,1,0:T(8,128)(2,1)S(1)} %all-gather.5), kind=kOutput, calls=%fused_computation.26 | convolution fusion | flops 2420834304 | bytes 21233664 | tf_op jit(solution)/shard_map/dot_general | solution.py:60
  362.1 35.5 %reduce-scatter.10.cloned.1.call-done = bf16[128,1536]{1,0:T(8,128)(2,1)} async-done(((bf16[128,6144]{1,0:T(8,128)(2,1)}), bf16[128,1536]{1,0:T(8,128)(2,1)}) %reduce-scatter.10.cloned.1.call-update) | async-done | bytes 393232 | tf_op jit(solution)/shard_map/reduce_scatter | solution.py:61
  397.6 1.2 bitcast_dynamic-update-slice_fusion.1
  398.8 1.3 collective-permute-start.2
  400.1 2.3 collective-permute-done.2
  403.4 39.9 %all-gather.26.cloned.1.call-done = bf16[128,6144]{1,0:T(8,128)(2,1)} async-done(((bf16[128,1536]{1,0:T(8,128)(2,1)}), bf16[128,6144]{1,0:T(8,128)(2,1)}) %all-gather.26.cloned.1.call-update) | async-done | bytes 1572880 | tf_op jit(solution)/shard_map/all_gather | solution.py:49
  443.3 14.0 %fusion.46 = bf16[128,1536]{1,0:T(8,128)(2,1)} fusion(bf16[128,6144]{1,0:T(8,128)(2,1)} %all-gather.26.cloned.1.call-done, bf16[1,1536,6144]{2,1,0:T(8,128)(2,1)} %param.9), kind=kOutput, calls=%fused_computation.32 | convolution fusion | flops 2416115712 | bytes 20840448 | tf_op jit(solution)/shard_map/dot_general | solution.py:52
  457.3 7.8 all-gather.7
  465.2 16.9 %all-reduce.12.cloned.1.call-done = bf16[128,1536]{1,0:T(8,128)(2,1)} async-done(((bf16[128,1536]{1,0:T(8,128)(2,1)}), bf16[128,1536]{1,0:T(8,128)(2,1)}) %all-reduce.12.cloned.1.call-update) | async-done | bytes 393232 | tf_op jit(solution)/shard_map/psum | solution.py:55
  482.1 10.7 %fusion.31 = bf16[128,6144]{1,0:T(8,128)(2,1)} fusion(bf16[1,1536,6144]{2,1,0:T(8,128)(2,1)} %param.8, bf16[128,1536]{1,0:T(8,128)(2,1)} %all-reduce.12.cloned.1.call-done, bf16[1,1,128,1536]{3,2,1,0:T(8,128)(2,1)S(1)} %all-gather.7), kind=kOutput, calls=%fused_computation.27 | convolution fusion | flops 2420834304 | bytes 21233664 | tf_op jit(solution)/shard_map/dot_general | solution.py:60
  493.6 34.8 %reduce-scatter.12.cloned.1.call-done = bf16[128,1536]{1,0:T(8,128)(2,1)} async-done(((bf16[128,6144]{1,0:T(8,128)(2,1)}), bf16[128,1536]{1,0:T(8,128)(2,1)}) %reduce-scatter.12.cloned.1.call-update) | async-done | bytes 393232 | tf_op jit(solution)/shard_map/reduce_scatter | solution.py:61
  528.4 1.4 bitcast_dynamic-update-slice_fusion
  529.8 1.3 collective-permute-start.3
  531.1 2.3 collective-permute-done.3
  533.4 0.8 bitcast_select_fusion.3
  534.3 3.1 constant_dynamic-slice_fusion.3
  539.2 35.2 %all-gather.28.cloned.1.call-done = bf16[128,6144]{1,0:T(8,128)(2,1)} async-done(((bf16[128,1536]{1,0:T(8,128)(2,1)}), bf16[128,6144]{1,0:T(8,128)(2,1)}) %all-gather.28.cloned.1.call-update) | async-done | bytes 1572880 | tf_op jit(solution)/shard_map/all_gather | solution.py:49
  574.3 14.0 %fusion.49 = bf16[128,1536]{1,0:T(8,128)(2,1)} fusion(bf16[128,6144]{1,0:T(8,128)(2,1)} %all-gather.28.cloned.1.call-done, bf16[1,1536,6144]{2,1,0:T(8,128)(2,1)} %param.9), kind=kOutput, calls=%fused_computation.33 | convolution fusion | flops 2416115712 | bytes 20840448 | tf_op jit(solution)/shard_map/dot_general | solution.py:52
  589.2 6.7 all-gather.9
  595.9 14.9 %fusion.61 = f32[1536,6144]{1,0:T(8,128)} fusion(bf16[1,128,6144]{2,1,0:T(8,128)(2,1)S(1)} %copy-done.2, bf16[1,1,128,1536]{3,2,1,0:T(8,128)(2,1)S(1)} %all-gather.1), kind=kOutput, calls=%fused_computation.78 | convolution fusion | flops 2417885184 | bytes 39714816 | tf_op jit(solution)/shard_map/dot_general | solution.py:65
  610.8 0.8 all-gather.32.cloned.1.call-done
  611.7 16.8 %fusion.59 = f32[1536,6144]{1,0:T(8,128)} fusion(bf16[1,1,128,6144]{3,2,1,0:T(8,128)(2,1)} %all-gather.32.cloned.1.call-done, bf16[128,1536]{1,0:T(8,128)(2,1)} %all-reduce.6.cloned.1.call-done, bf16[1,1,128,1536]{3,2,1,0:T(8,128)(2,1)S(1)} %all-gather.1), kind=kOutput, calls=%fused_computation.76 | convolution fusion | flops 2420047872 | bytes 40108032 | tf_op jit(solution)/shard_map/dot_general | solution.py:68
  628.5 14.9 %fusion.121 = f32[1536,6144]{1,0:T(8,128)} fusion(bf16[128,6144]{1,0:T(8,128)(2,1)S(1)} %copy-done.3, bf16[1,1,128,1536]{3,2,1,0:T(8,128)(2,1)S(1)} %copy-done.7), kind=kOutput, calls=%fused_computation.142 | convolution fusion | flops 2417885184 | bytes 39714816 | tf_op jit(solution)/shard_map/dot_general | solution.py:65
  643.4 6.2 all-gather.34.cloned.1.call-done
  649.6 16.7 %fusion.57 = f32[1536,6144]{1,0:T(8,128)} fusion(bf16[1,1,128,6144]{3,2,1,0:T(8,128)(2,1)} %all-gather.34.cloned.1.call-done, bf16[128,1536]{1,0:T(8,128)(2,1)S(1)} %copy-done.20, bf16[1,1,128,1536]{3,2,1,0:T(8,128)(2,1)S(1)} %copy-done.7), kind=kOutput, calls=%fused_computation.74 | convolution fusion | flops 2420047872 | bytes 40108032 | tf_op jit(solution)/shard_map/dot_general | solution.py:68
  666.3 15.4 %fusion.123 = f32[1536,6144]{1,0:T(8,128)} fusion(bf16[128,6144]{1,0:T(8,128)(2,1)S(1)} %copy-done.4, bf16[1,1,128,1536]{3,2,1,0:T(8,128)(2,1)S(1)} %copy-done.9), kind=kOutput, calls=%fused_computation.143 | convolution fusion | flops 2417885184 | bytes 39714816 | tf_op jit(solution)/shard_map/dot_general | solution.py:65
  681.6 5.9 all-gather.36.cloned.1.call-done
  687.5 16.6 %fusion.55 = f32[1536,6144]{1,0:T(8,128)} fusion(bf16[1,1,128,6144]{3,2,1,0:T(8,128)(2,1)} %all-gather.36.cloned.1.call-done, bf16[128,1536]{1,0:T(8,128)(2,1)S(1)} %copy-done.21, bf16[1,1,128,1536]{3,2,1,0:T(8,128)(2,1)S(1)} %copy-done.9), kind=kOutput, calls=%fused_computation.72 | convolution fusion | flops 2420047872 | bytes 40108032 | tf_op jit(solution)/shard_map/dot_general | solution.py:68
  704.1 14.9 %fusion.125 = f32[1536,6144]{1,0:T(8,128)} fusion(bf16[128,6144]{1,0:T(8,128)(2,1)S(1)} %copy-done.5, bf16[1,1,128,1536]{3,2,1,0:T(8,128)(2,1)S(1)} %copy-done.11), kind=kOutput, calls=%fused_computation.144 | convolution fusion | flops 2417885184 | bytes 39714816 | tf_op jit(solution)/shard_map/dot_general | solution.py:65
  719.0 5.9 all-gather.38.cloned.1.call-done
  724.8 16.4 %fusion.53 = f32[1536,6144]{1,0:T(8,128)} fusion(bf16[1,1,128,6144]{3,2,1,0:T(8,128)(2,1)} %all-gather.38.cloned.1.call-done, bf16[128,1536]{1,0:T(8,128)(2,1)S(1)} %copy-done.22, bf16[1,1,128,1536]{3,2,1,0:T(8,128)(2,1)S(1)} %copy-done.11), kind=kOutput, calls=%fused_computation.70 | convolution fusion | flops 2420047872 | bytes 40108032 | tf_op jit(solution)/shard_map/dot_general | solution.py:68
  741.2 0.9 copy.17
  742.1 25.1 %fusion.1 = bf16[1,1536,6144]{2,1,0:T(8,128)(2,1)} fusion(bf16[128,6144]{1,0:T(8,128)(2,1)S(1)} %copy-done.1, f32[1536,6144]{1,0:T(8,128)} %fusion.125, f32[1536,6144]{1,0:T(8,128)} %fusion.123, f32[1536,6144]{1,0:T(8,128)} %fusion.121, f32[1536,6144]{1,0:T(8,128)} %fusion.61, pred[]{:T(512)S(6)} %and.20, pred[]{:T(512)S(6)} %and.19, pred[]{:T(512)S(6)} %and.18, ...), kind=kOutput, calls=%fused_computation.3 | convolution fusion | flops 2512257024 | bytes 171835392 | tf_op jit(solution)/shard_map/dot_general | solution.py:65
  767.3 10.8 %fusion.34 = bf16[128,6144]{1,0:T(8,128)(2,1)} fusion(bf16[1,1536,6144]{2,1,0:T(8,128)(2,1)} %param.8, bf16[128,1536]{1,0:T(8,128)(2,1)} %all-reduce.14.cloned.1.call-done, bf16[1,1,128,1536]{3,2,1,0:T(8,128)(2,1)S(1)} %copy-done.15), kind=kOutput, calls=%fused_computation.28 | convolution fusion | flops 2420834304 | bytes 21233664 | tf_op jit(solution)/shard_map/dot_general | solution.py:60
  778.1 12.7 %all-gather.40.cloned.1.call-done = bf16[1,1,128,6144]{3,2,1,0:T(8,128)(2,1)} async-done(((bf16[1,1,128,1536]{3,2,1,0:T(8,128)(2,1)}), bf16[1,1,128,6144]{3,2,1,0:T(8,128)(2,1)}) %all-gather.40.cloned.1.call-update) | async-done | bytes 1572880 | tf_op jit(solution)/shard_map/all_gather | solution.py:50
  790.9 25.9 %fusion = bf16[1,1536,6144]{2,1,0:T(8,128)(2,1)} fusion(f32[1536,6144]{1,0:T(8,128)} %fusion.53, f32[1536,6144]{1,0:T(8,128)} %fusion.55, f32[1536,6144]{1,0:T(8,128)} %fusion.57, f32[1536,6144]{1,0:T(8,128)} %fusion.59, pred[]{:T(512)S(6)} %and.20, pred[]{:T(512)S(6)} %and.19, pred[]{:T(512)S(6)} %and.18, pred[]{:T(512)S(6)} %and.17, pred[]{:T(512)S(6)} %and.16, ...), kind=kOutput, calls=%fused_computation.2 | convolution fusion | flops 2514419712 | bytes 172228608 | tf_op jit(solution)/shard_map/dot_general | solution.py:68
  816.8 10.6 %reduce-scatter.14.cloned.1.call-done = bf16[128,1536]{1,0:T(8,128)(2,1)} async-done(((bf16[128,6144]{1,0:T(8,128)(2,1)}), bf16[128,1536]{1,0:T(8,128)(2,1)}) %reduce-scatter.14.cloned.1.call-update) | async-done | bytes 393232 | tf_op jit(solution)/shard_map/reduce_scatter | solution.py:61
  827.3 1.1 fusion.130
  828.5 0.9 copy-done.18
  (94 shorter events, 7.0 us)
Async XLA Ops:
  7.2 56.8 %copy-start.16 = (bf16[1,2,64,1536]{3,2,1,0:T(8,128)(2,1)S(1)}, bf16[1,2,64,1536]{3,2,1,0:T(8,128)(2,1)}, u32[]{:S(2)}) copy-start(bf16[1,2,64,1536]{3,2,1,0:T(8,128)(2,1)} %param.7) | copy-start | bytes 1179652
  7.2 42.7 %all-gather.30.cloned.1.call-start = ((), (), s32[]{:S(2)}) async-start(), calls=%async_computation.19 | async-start | bytes 1966080 | tf_op jit(solution)/shard_map/all_gather | solution.py:49
  9.1 80.4 %all-reduce.6.cloned.1.call-start = ((), (), s32[]{:S(2)}) async-start(), calls=%async_computation.5 | async-start | bytes 786432 | tf_op jit(solution)/shard_map/psum | solution.py:55
  63.9 71.9 %copy-start = (bf16[2,128,1536]{2,1,0:T(8,128)(2,1)S(1)}, bf16[2,128,1536]{2,1,0:T(8,128)(2,1)}, u32[]{:S(2)}) copy-start(bf16[2,128,1536]{2,1,0:T(8,128)(2,1)} %param.5) | copy-start | bytes 2359300
  63.9 71.9 %reduce-scatter.6.cloned.1.call-start = ((), (), s32[]{:S(2)}) async-start(), calls=%async_computation.6 | async-start | bytes 1966080 | tf_op jit(solution)/shard_map/reduce_scatter | solution.py:61
  100.2 81.4 %all-gather.22.cloned.1.call-start = ((), (), s32[]{:S(2)}) async-start(), calls=%async_computation.7 | async-start | bytes 1966080 | tf_op jit(solution)/shard_map/all_gather | solution.py:49
  137.0 3.6 collective-permute-start
  141.4 79.0 %all-reduce.8.cloned.1.call-start = ((), (), s32[]{:S(2)}) async-start(), calls=%async_computation.8 | async-start | bytes 786432 | tf_op jit(solution)/shard_map/psum | solution.py:55
  195.5 71.2 %copy-start.12 = (bf16[128,1536]{1,0:T(8,128)(2,1)S(1)}, bf16[128,1536]{1,0:T(8,128)(2,1)}, u32[]{:S(2)}) copy-start(bf16[128,1536]{1,0:T(8,128)(2,1)} %bitcast_select_fusion.6) | copy-start | bytes 1179652
  195.5 71.2 %reduce-scatter.8.cloned.1.call-start = ((), (), s32[]{:S(2)}) async-start(), calls=%async_computation.9 | async-start | bytes 1966080 | tf_op jit(solution)/shard_map/reduce_scatter | solution.py:61
  203.8 122.6 %copy-start.6 = (bf16[1,1,128,1536]{3,2,1,0:T(8,128)(2,1)}, bf16[1,1,128,1536]{3,2,1,0:T(8,128)(2,1)S(1)}, u32[]{:S(2)}) copy-start(bf16[1,1,128,1536]{3,2,1,0:T(8,128)(2,1)S(1)} %all-gather.3) | copy-start | bytes 1179652
  231.1 81.3 %all-gather.24.cloned.1.call-start = ((), (), s32[]{:S(2)}) async-start(), calls=%async_computation.10 | async-start | bytes 1966080 | tf_op jit(solution)/shard_map/all_gather | solution.py:49
  267.9 3.6 collective-permute-start.1
  272.3 79.0 %all-reduce.10.cloned.1.call-start = ((), (), s32[]{:S(2)}) async-start(), calls=%async_computation.11 | async-start | bytes 786432 | tf_op jit(solution)/shard_map/psum | solution.py:55
  326.4 71.2 %copy-start.13 = (bf16[128,1536]{1,0:T(8,128)(2,1)S(1)}, bf16[128,1536]{1,0:T(8,128)(2,1)}, u32[]{:S(2)}) copy-start(bf16[128,1536]{1,0:T(8,128)(2,1)} %bitcast_select_fusion.5) | copy-start | bytes 1179652
  326.4 71.2 %reduce-scatter.10.cloned.1.call-start = ((), (), s32[]{:S(2)}) async-start(), calls=%async_computation.12 | async-start | bytes 1966080 | tf_op jit(solution)/shard_map/reduce_scatter | solution.py:61
  334.7 122.5 %copy-start.8 = (bf16[1,1,128,1536]{3,2,1,0:T(8,128)(2,1)}, bf16[1,1,128,1536]{3,2,1,0:T(8,128)(2,1)S(1)}, u32[]{:S(2)}) copy-start(bf16[1,1,128,1536]{3,2,1,0:T(8,128)(2,1)S(1)} %all-gather.5) | copy-start | bytes 1179652
  362.0 81.3 %all-gather.26.cloned.1.call-start = ((), (), s32[]{:S(2)}) async-start(), calls=%async_computation.13 | async-start | bytes 1966080 | tf_op jit(solution)/shard_map/all_gather | solution.py:49
  398.8 3.6 collective-permute-start.2
  403.2 78.9 %all-reduce.12.cloned.1.call-start = ((), (), s32[]{:S(2)}) async-start(), calls=%async_computation.14 | async-start | bytes 786432 | tf_op jit(solution)/shard_map/psum | solution.py:55
  457.3 71.1 %reduce-scatter.12.cloned.1.call-start = ((), (), s32[]{:S(2)}) async-start(), calls=%async_computation.15 | async-start | bytes 1966080 | tf_op jit(solution)/shard_map/reduce_scatter | solution.py:61
  465.2 16.9 %copy-start.10 = (bf16[1,1,128,1536]{3,2,1,0:T(8,128)(2,1)}, bf16[1,1,128,1536]{3,2,1,0:T(8,128)(2,1)S(1)}, u32[]{:S(2)}) copy-start(bf16[1,1,128,1536]{3,2,1,0:T(8,128)(2,1)S(1)} %all-gather.7) | copy-start | bytes 1179652
  492.7 103.2 %copy-start.2 = (bf16[1,128,6144]{2,1,0:T(8,128)(2,1)S(1)}, bf16[1,128,6144]{2,1,0:T(8,128)(2,1)}, u32[]{:S(2)}) copy-start(bf16[1,128,6144]{2,1,0:T(8,128)(2,1)} %all-gather.30.cloned.1.call-done) | copy-start | bytes 4718596
  492.8 81.5 %all-gather.28.cloned.1.call-start = ((), (), s32[]{:S(2)}) async-start(), calls=%async_computation.16 | async-start | bytes 1966080 | tf_op jit(solution)/shard_map/all_gather | solution.py:49
  529.8 3.6 collective-permute-start.3
  534.2 55.0 %copy-start.19 = (bf16[1,1,64,1536]{3,2,1,0:T(8,128)(2,1)S(1)}, bf16[1,1,64,1536]{3,2,1,0:T(8,128)(2,1)}, u32[]{:S(2)}) copy-start(bf16[1,1,64,1536]{3,2,1,0:T(8,128)(2,1)} %get-tuple-element.16) | copy-start | bytes 589828
  534.2 77.5 %all-gather.32.cloned.1.call-start = ((), (), s32[]{:S(2)}) async-start(), calls=%async_computation.20 | async-start | bytes 1966080 | tf_op jit(solution)/shard_map/all_gather | solution.py:50
  537.4 112.2 %all-gather.34.cloned.1.call-start = ((), (), s32[]{:S(2)}) async-start(), calls=%async_computation.21 | async-start | bytes 1966080 | tf_op jit(solution)/shard_map/all_gather | solution.py:50
  538.0 149.5 %all-gather.36.cloned.1.call-start = ((), (), s32[]{:S(2)}) async-start(), calls=%async_computation.22 | async-start | bytes 1966080 | tf_op jit(solution)/shard_map/all_gather | solution.py:50
  538.5 186.3 %all-gather.38.cloned.1.call-start = ((), (), s32[]{:S(2)}) async-start(), calls=%async_computation.23 | async-start | bytes 1966080 | tf_op jit(solution)/shard_map/all_gather | solution.py:50
  539.1 228.1 %all-reduce.14.cloned.1.call-start = ((), (), s32[]{:S(2)}) async-start(), calls=%async_computation.17 | async-start | bytes 786432 | tf_op jit(solution)/shard_map/psum | solution.py:55
  588.4 202.5 %all-gather.40.cloned.1.call-start = ((), (), s32[]{:S(2)}) async-start(), calls=%async_computation.24 | async-start | bytes 1966080 | tf_op jit(solution)/shard_map/all_gather | solution.py:50
  589.1 238.2 %reduce-scatter.14.cloned.1.call-start = ((), (), s32[]{:S(2)}) async-start(), calls=%async_computation.18 | async-start | bytes 1966080 | tf_op jit(solution)/shard_map/reduce_scatter | solution.py:61
  610.8 17.7 %copy-start.3 = (bf16[128,6144]{1,0:T(8,128)(2,1)S(1)}, bf16[128,6144]{1,0:T(8,128)(2,1)}, u32[]{:S(2)}) copy-start(bf16[128,6144]{1,0:T(8,128)(2,1)} %all-gather.22.cloned.1.call-done) | copy-start | bytes 4718596
  610.8 17.7 %copy-start.7 = (bf16[1,1,128,1536]{3,2,1,0:T(8,128)(2,1)S(1)}, bf16[1,1,128,1536]{3,2,1,0:T(8,128)(2,1)}, u32[]{:S(2)}) copy-start(bf16[1,1,128,1536]{3,2,1,0:T(8,128)(2,1)} %copy-done.6) | copy-start | bytes 1179652
  628.5 21.1 %copy-start.20 = (bf16[128,1536]{1,0:T(8,128)(2,1)S(1)}, bf16[128,1536]{1,0:T(8,128)(2,1)}, u32[]{:S(2)}) copy-start(bf16[128,1536]{1,0:T(8,128)(2,1)} %all-reduce.8.cloned.1.call-done) | copy-start | bytes 1179652
  643.4 22.9 %copy-start.4 = (bf16[128,6144]{1,0:T(8,128)(2,1)S(1)}, bf16[128,6144]{1,0:T(8,128)(2,1)}, u32[]{:S(2)}) copy-start(bf16[128,6144]{1,0:T(8,128)(2,1)} %all-gather.24.cloned.1.call-done) | copy-start | bytes 4718596
  643.4 22.9 %copy-start.9 = (bf16[1,1,128,1536]{3,2,1,0:T(8,128)(2,1)S(1)}, bf16[1,1,128,1536]{3,2,1,0:T(8,128)(2,1)}, u32[]{:S(2)}) copy-start(bf16[1,1,128,1536]{3,2,1,0:T(8,128)(2,1)} %copy-done.8) | copy-start | bytes 1179652
  666.3 21.2 %copy-start.21 = (bf16[128,1536]{1,0:T(8,128)(2,1)S(1)}, bf16[128,1536]{1,0:T(8,128)(2,1)}, u32[]{:S(2)}) copy-start(bf16[128,1536]{1,0:T(8,128)(2,1)} %all-reduce.10.cloned.1.call-done) | copy-start | bytes 1179652
  681.6 22.5 %copy-start.5 = (bf16[128,6144]{1,0:T(8,128)(2,1)S(1)}, bf16[128,6144]{1,0:T(8,128)(2,1)}, u32[]{:S(2)}) copy-start(bf16[128,6144]{1,0:T(8,128)(2,1)} %all-gather.26.cloned.1.call-done) | copy-start | bytes 4718596
  681.6 22.5 %copy-start.11 = (bf16[1,1,128,1536]{3,2,1,0:T(8,128)(2,1)S(1)}, bf16[1,1,128,1536]{3,2,1,0:T(8,128)(2,1)}, u32[]{:S(2)}) copy-start(bf16[1,1,128,1536]{3,2,1,0:T(8,128)(2,1)} %copy-done.10) | copy-start | bytes 1179652
  704.1 20.7 %copy-start.22 = (bf16[128,1536]{1,0:T(8,128)(2,1)S(1)}, bf16[128,1536]{1,0:T(8,128)(2,1)}, u32[]{:S(2)}) copy-start(bf16[128,1536]{1,0:T(8,128)(2,1)} %all-reduce.12.cloned.1.call-done) | copy-start | bytes 1179652
  719.0 23.2 %copy-start.1 = (bf16[128,6144]{1,0:T(8,128)(2,1)S(1)}, bf16[128,6144]{1,0:T(8,128)(2,1)}, u32[]{:S(2)}) copy-start(bf16[128,6144]{1,0:T(8,128)(2,1)} %all-gather.28.cloned.1.call-done) | copy-start | bytes 4718596
  719.0 23.2 %copy-start.15 = (bf16[1,1,128,1536]{3,2,1,0:T(8,128)(2,1)S(1)}, bf16[1,1,128,1536]{3,2,1,0:T(8,128)(2,1)}, u32[]{:S(2)}) copy-start(bf16[1,1,128,1536]{3,2,1,0:T(8,128)(2,1)} %all-gather.9) | copy-start | bytes 1179652
  767.2 23.6 %copy-start.23 = (bf16[128,1536]{1,0:T(8,128)(2,1)S(1)}, bf16[128,1536]{1,0:T(8,128)(2,1)}, u32[]{:S(2)}) copy-start(bf16[128,1536]{1,0:T(8,128)(2,1)} %all-reduce.14.cloned.1.call-done) | copy-start | bytes 1179652
  778.1 49.2 %copy-start.14 = (bf16[128,1536]{1,0:T(8,128)(2,1)S(1)}, bf16[128,1536]{1,0:T(8,128)(2,1)}, u32[]{:S(2)}) copy-start(bf16[128,1536]{1,0:T(8,128)(2,1)} %bitcast_select_fusion.3) | copy-start | bytes 1179652
  778.1 49.2 %copy-start.17 = (bf16[1,2,128,1536]{3,2,1,0:T(8,128)(2,1)S(1)}, bf16[1,2,128,1536]{3,2,1,0:T(8,128)(2,1)}, u32[]{:S(2)}) copy-start(bf16[1,2,128,1536]{3,2,1,0:T(8,128)(2,1)} %copy.17) | copy-start | bytes 2359300
  828.5 0.9 copy-start.18
Sparse Core Ops, SparseCore 0:
  10.1 39.7 all-gather.29
  64.0 25.3 all-reduce.5
  100.3 35.4 reduce-scatter.5
  141.5 39.9 all-gather.21
  195.6 24.7 all-reduce.7
  231.2 35.4 reduce-scatter.7
  272.4 39.9 all-gather.23
  326.5 24.7 all-reduce.9
  362.1 35.4 reduce-scatter.9
  403.3 39.9 all-gather.25
  457.4 24.6 all-reduce.11
  492.9 35.4 reduce-scatter.11
  534.3 39.9 all-gather.27
  575.7 35.8 all-gather.31
  613.6 35.8 all-gather.33
  651.6 35.8 all-gather.35
  688.9 35.8 all-gather.37
  727.0 24.6 all-reduce.13
  753.8 37.0 all-gather.39
  793.0 34.2 reduce-scatter.13
where the time goes:
time: 843 us; the launch traced here: 836 us
  waiting for transfers between devices  456 us (54%)
  matrix products  301 us (36%)
  blocking collectives  40.5 us (5%)
  between operations  14.8 us (2%)
  other arithmetic  9.16 us (1%)
  local copies, waits for them, and re-layouts  8.44 us (1%)
    all_gather x5, waiting for transfers between devices, on_device(): lax.all_gather(current, 'tensor', axis=1, tiled=True)  195 us
    reduce_scatter x5, waiting for transfers between devices, on_device(): lax.psum_scatter(partial_value.astype(jnp.bfloat16), 'tensor', scatter_di...  152 us
    dot_general x5, matrix products, on_device(): lax.dot_general(head_delta, input_cols, contract, preferred_element_type=...  92.4 us
    dot_general x5, matrix products, on_device(): lax.dot_general(activated, grad_cols, contract, preferred_element_type=jn...  85.1 us
    dot_general x5, matrix products, on_device(): lax.dot_general(grad_cols, local_out, (((1,), (1,)), ((), ())), preferred...  69.8 us
    psum x5, waiting for transfers between devices, on_device(): lax.psum(head_part.astype(jnp.bfloat16), 'dp').astype(jnp.float32)  65.3 us
    dot_general x5, matrix products, on_device(): jnp.dot(head_delta, local_in, preferred_element_type=jnp.float32)  53.6 us
    all_gather x5, blocking collectives, on_device(): pre_all = lax.all_gather(pre_local, 'dp', axis=0, tiled=True)  40.5 us
  transfers between devices with their start and end apart: 24, of which 23 were waited for; matrix products, arithmetic and copies ran while one was open for 25% of the time, Pallas kernels for 0%

commit v1 on v0

--- a/solution.py
+++ b/solution.py
@@ -52,7 +52,9 @@
         head_part = lax.dot_general(
             grad_cols, local_out, (((1,), (1,)), ((), ())), preferred_element_type=jnp.float32
         )
-        head_grad = lax.psum(head_part.astype(jnp.bfloat16), "dp").astype(jnp.float32)
+        head_grad = jnp.sum(lax.all_gather(head_part.astype(jnp.bfloat16), "dp"), axis=0).astype(
+            jnp.float32
+        )
         pre_all = lax.all_gather(pre_local, "dp", axis=0, tiled=True)
         activ, slope = gelu_pair(pre_all.astype(jnp.float32))
         head_delta = (head_grad * slope).astype(jnp.bfloat16)

time: 843 us -> 778 us (0.923)
  the two profiles are of different devices: /device:TPU:0 before, /device:TPU:1 now
where the time goes in v1:
time: 778 us; the launch traced here: 771 us
  waiting for transfers between devices  328 us (42%)
  matrix products  313 us (40%)
  blocking collectives  80.9 us (10%)
  between operations  14.7 us (2%)
  other arithmetic  13.2 us (2%)
  starting transfers between devices  12.6 us (2%)
  local copies, waits for them, and re-layouts  8.74 us (1%)
    reduce_scatter x5, waiting for transfers between devices, on_device(): lax.psum_scatter(partial_value.astype(jnp.bfloat16), 'tensor', scatter_di...  141 us
    all_gather x5, waiting for transfers between devices, on_device(): lax.all_gather(current, 'tensor', axis=1, tiled=True)  134 us
    dot_general x5, matrix products, on_device(): lax.dot_general(head_delta, input_cols, contract, preferred_element_type=...  100 us
    dot_general x5, matrix products, on_device(): lax.dot_general(activated, grad_cols, contract, preferred_element_type=jn...  91.6 us
    dot_general x5, matrix products, on_device(): lax.dot_general(grad_cols, local_out, (((1,), (1,)), ((), ())), preferred...  67.5 us
    dot_general x5, matrix products, on_device(): jnp.dot(head_delta, local_in, preferred_element_type=jnp.float32)  53.7 us
    all_gather x5, blocking collectives, on_device(): lax.all_gather(head_part.astype(jnp.bfloat16), 'dp')  49.8 us
    all_gather x5, blocking collectives, on_device(): pre_all = lax.all_gather(pre_local, 'dp', axis=0, tiled=True)  31.1 us
  transfers between devices with their start and end apart: 19, of which 18 were waited for; matrix products, arithmetic and copies ran while one was open for 29% of the time, Pallas kernels for 0%

profile of v1, /device:TPU:1, one launch (start us, length us, event | category | flops | bytes accessed | tf_op | source)
XLA Modules:
  0.0 771.1 jit_solution(14199324521474197440)
XLA Ops:
  7.2 1.8 constant_dynamic-slice_fusion.13
  9.1 2.1 constant_dynamic-slice_fusion.4
  11.2 7.2 all-gather.2
  18.4 29.9 %all-gather.35.cloned.1.call-done = bf16[1,128,6144]{2,1,0:T(8,128)(2,1)} async-done(((bf16[1,128,1536]{2,1,0:T(8,128)(2,1)}), bf16[1,128,6144]{2,1,0:T(8,128)(2,1)}) %all-gather.35.cloned.1.call-update) | async-done | bytes 1572880 | tf_op jit(solution)/shard_map/all_gather | solution.py:49
  48.4 13.2 %fusion.37 = bf16[128,1536]{1,0:T(8,128)(2,1)S(1)} fusion(bf16[1,1536,6144]{2,1,0:T(8,128)(2,1)} %param.9, bf16[1,128,6144]{2,1,0:T(8,128)(2,1)} %all-gather.35.cloned.1.call-done), kind=kOutput, calls=%fused_computation.29 | convolution fusion | flops 2416115712 | bytes 20840448 | tf_op jit(solution)/shard_map/dot_general | solution.py:52
  61.6 9.9 %all-gather.1 = bf16[256,1536]{1,0:T(8,128)(2,1)S(1)} all-gather(bf16[128,1536]{1,0:T(8,128)(2,1)S(1)} %fusion.37), channel_id=3, replica_groups=mesh['pipe'=4,'dp'=2,'tensor'=4] {'dp'}, dimensions={0}, use_global_device_ids=true | all-gather | bytes 1179648 | tf_op jit(solution)/shard_map/all_gather | solution.py:55
  71.7 10.7 %fusion.22 = bf16[128,6144]{1,0:T(8,128)(2,1)} fusion(bf16[1,1536,6144]{2,1,0:T(8,128)(2,1)} %param.8, bf16[128,1536]{1,0:T(8,128)(2,1)S(1)} %reduce_sum.60, bf16[1,1,128,1536]{3,2,1,0:T(8,128)(2,1)S(1)} %all-gather.2), kind=kOutput, calls=%fused_computation.24 | convolution fusion | flops 2420834304 | bytes 21233664 | tf_op jit(solution)/shard_map/dot_general | solution.py:62
  82.4 36.7 %reduce-scatter.6.cloned.1.call-done = bf16[128,1536]{1,0:T(8,128)(2,1)} async-done(((bf16[128,6144]{1,0:T(8,128)(2,1)}), bf16[128,1536]{1,0:T(8,128)(2,1)}) %reduce-scatter.6.cloned.1.call-update) | async-done | bytes 393232 | tf_op jit(solution)/shard_map/reduce_scatter | solution.py:63
  119.2 1.1 bitcast_dynamic-update-slice_fusion.3
  120.4 3.0 collective-permute-start
  123.4 6.8 collective-permute-done
  131.0 5.4 all-gather.5
  136.4 28.3 %all-gather.27.cloned.1.call-done = bf16[128,6144]{1,0:T(8,128)(2,1)} async-done(((bf16[128,1536]{1,0:T(8,128)(2,1)}), bf16[128,6144]{1,0:T(8,128)(2,1)}) %all-gather.27.cloned.1.call-update) | async-done | bytes 1572880 | tf_op jit(solution)/shard_map/all_gather | solution.py:49
  164.7 14.0 %fusion.40 = bf16[128,1536]{1,0:T(8,128)(2,1)} fusion(bf16[128,6144]{1,0:T(8,128)(2,1)} %all-gather.27.cloned.1.call-done, bf16[1,1536,6144]{2,1,0:T(8,128)(2,1)} %param.9), kind=kOutput, calls=%fused_computation.30 | convolution fusion | flops 2416115712 | bytes 20840448 | tf_op jit(solution)/shard_map/dot_general | solution.py:52
  178.7 10.1 %all-gather.4 = bf16[256,1536]{1,0:T(8,128)(2,1)S(1)} all-gather(bf16[128,1536]{1,0:T(8,128)(2,1)} %fusion.40), channel_id=6, replica_groups=mesh['pipe'=4,'dp'=2,'tensor'=4] {'dp'}, dimensions={0}, use_global_device_ids=true | all-gather | bytes 1179648 | tf_op jit(solution)/shard_map/all_gather | solution.py:55
  188.8 1.0 reduce_sum.61
  189.8 10.7 %fusion.25 = bf16[128,6144]{1,0:T(8,128)(2,1)} fusion(bf16[1,1536,6144]{2,1,0:T(8,128)(2,1)} %param.8, bf16[128,1536]{1,0:T(8,128)(2,1)} %reduce_sum.61, bf16[1,1,128,1536]{3,2,1,0:T(8,128)(2,1)S(1)} %all-gather.5), kind=kOutput, calls=%fused_computation.25 | convolution fusion | flops 2420834304 | bytes 21233664 | tf_op jit(solution)/shard_map/dot_general | solution.py:62
  200.6 36.7 %reduce-scatter.8.cloned.1.call-done = bf16[128,1536]{1,0:T(8,128)(2,1)} async-done(((bf16[128,6144]{1,0:T(8,128)(2,1)}), bf16[128,1536]{1,0:T(8,128)(2,1)}) %reduce-scatter.8.cloned.1.call-update) | async-done | bytes 393232 | tf_op jit(solution)/shard_map/reduce_scatter | solution.py:63
  237.3 1.2 bitcast_dynamic-update-slice_fusion.2
  238.5 3.0 collective-permute-start.1
  241.4 6.8 collective-permute-done.1
  249.1 5.4 all-gather.8
  254.6 28.2 %all-gather.29.cloned.1.call-done = bf16[128,6144]{1,0:T(8,128)(2,1)} async-done(((bf16[128,1536]{1,0:T(8,128)(2,1)}), bf16[128,6144]{1,0:T(8,128)(2,1)}) %all-gather.29.cloned.1.call-update) | async-done | bytes 1572880 | tf_op jit(solution)/shard_map/all_gather | solution.py:49
  282.8 14.0 %fusion.43 = bf16[128,1536]{1,0:T(8,128)(2,1)} fusion(bf16[128,6144]{1,0:T(8,128)(2,1)} %all-gather.29.cloned.1.call-done, bf16[1,1536,6144]{2,1,0:T(8,128)(2,1)} %param.9), kind=kOutput, calls=%fused_computation.31 | convolution fusion | flops 2416115712 | bytes 20840448 | tf_op jit(solution)/shard_map/dot_general | solution.py:52
  296.8 10.1 %all-gather.7 = bf16[256,1536]{1,0:T(8,128)(2,1)S(1)} all-gather(bf16[128,1536]{1,0:T(8,128)(2,1)} %fusion.43), channel_id=9, replica_groups=mesh['pipe'=4,'dp'=2,'tensor'=4] {'dp'}, dimensions={0}, use_global_device_ids=true | all-gather | bytes 1179648 | tf_op jit(solution)/shard_map/all_gather | solution.py:55
  306.9 1.0 reduce_sum.62
  307.9 10.7 %fusion.28 = bf16[128,6144]{1,0:T(8,128)(2,1)} fusion(bf16[1,1536,6144]{2,1,0:T(8,128)(2,1)} %param.8, bf16[128,1536]{1,0:T(8,128)(2,1)} %reduce_sum.62, bf16[1,1,128,1536]{3,2,1,0:T(8,128)(2,1)S(1)} %all-gather.8), kind=kOutput, calls=%fused_computation.26 | convolution fusion | flops 2420834304 | bytes 21233664 | tf_op jit(solution)/shard_map/dot_general | solution.py:62
  318.7 36.7 %reduce-scatter.10.cloned.1.call-done = bf16[128,1536]{1,0:T(8,128)(2,1)} async-done(((bf16[128,6144]{1,0:T(8,128)(2,1)}), bf16[128,1536]{1,0:T(8,128)(2,1)}) %reduce-scatter.10.cloned.1.call-update) | async-done | bytes 393232 | tf_op jit(solution)/shard_map/reduce_scatter | solution.py:63
  355.4 1.2 bitcast_dynamic-update-slice_fusion.1
  356.6 3.0 collective-permute-start.2
  359.6 6.5 collective-permute-done.2
  367.0 5.8 all-gather.11
  372.7 27.9 %all-gather.31.cloned.1.call-done = bf16[128,6144]{1,0:T(8,128)(2,1)} async-done(((bf16[128,1536]{1,0:T(8,128)(2,1)}), bf16[128,6144]{1,0:T(8,128)(2,1)}) %all-gather.31.cloned.1.call-update) | async-done | bytes 1572880 | tf_op jit(solution)/shard_map/all_gather | solution.py:49
  400.6 13.2 %fusion.46 = bf16[128,1536]{1,0:T(8,128)(2,1)S(1)} fusion(bf16[128,6144]{1,0:T(8,128)(2,1)} %all-gather.31.cloned.1.call-done, bf16[1,1536,6144]{2,1,0:T(8,128)(2,1)} %param.9), kind=kOutput, calls=%fused_computation.32 | convolution fusion | flops 2416115712 | bytes 20840448 | tf_op jit(solution)/shard_map/dot_general | solution.py:52
  413.8 9.8 %all-gather.10 = bf16[256,1536]{1,0:T(8,128)(2,1)S(1)} all-gather(bf16[128,1536]{1,0:T(8,128)(2,1)S(1)} %fusion.46), channel_id=12, replica_groups=mesh['pipe'=4,'dp'=2,'tensor'=4] {'dp'}, dimensions={0}, use_global_device_ids=true | all-gather | bytes 1179648 | tf_op jit(solution)/shard_map/all_gather | solution.py:55
  423.6 1.0 reduce_sum.63
  424.6 10.9 %fusion.31 = bf16[128,6144]{1,0:T(8,128)(2,1)} fusion(bf16[1,1536,6144]{2,1,0:T(8,128)(2,1)} %param.8, bf16[128,1536]{1,0:T(8,128)(2,1)} %reduce_sum.63, bf16[1,1,128,1536]{3,2,1,0:T(8,128)(2,1)} %all-gather.11), kind=kOutput, calls=%fused_computation.27 | convolution fusion | flops 2420834304 | bytes 21233664 | tf_op jit(solution)/shard_map/dot_general | solution.py:62
  435.6 3.0 constant_dynamic-slice_fusion.3
  441.3 31.0 %reduce-scatter.12.cloned.1.call-done = bf16[128,1536]{1,0:T(8,128)(2,1)} async-done(((bf16[128,6144]{1,0:T(8,128)(2,1)}), bf16[128,1536]{1,0:T(8,128)(2,1)}) %reduce-scatter.12.cloned.1.call-update) | async-done | bytes 393232 | tf_op jit(solution)/shard_map/reduce_scatter | solution.py:63
  472.3 1.4 bitcast_dynamic-update-slice_fusion
  473.7 3.0 collective-permute-start.3
  476.7 6.5 collective-permute-done.3
  484.7 7.3 all-gather.14
  492.0 14.8 %fusion.61 = f32[1536,6144]{1,0:T(8,128)} fusion(bf16[1,128,6144]{2,1,0:T(8,128)(2,1)S(1)} %copy-done.2, bf16[1,1,128,1536]{3,2,1,0:T(8,128)(2,1)S(1)} %all-gather.2), kind=kOutput, calls=%fused_computation.78 | convolution fusion | flops 2417885184 | bytes 39714816 | tf_op jit(solution)/shard_map/dot_general | solution.py:67
  506.7 2.6 all-gather.37.cloned.1.call-done
  509.3 16.8 %fusion.59 = f32[1536,6144]{1,0:T(8,128)} fusion(bf16[1,1,128,6144]{3,2,1,0:T(8,128)(2,1)} %all-gather.37.cloned.1.call-done, bf16[128,1536]{1,0:T(8,128)(2,1)} %copy-done.15, bf16[1,1,128,1536]{3,2,1,0:T(8,128)(2,1)S(1)} %all-gather.2), kind=kOutput, calls=%fused_computation.76 | convolution fusion | flops 2420047872 | bytes 40108032 | tf_op jit(solution)/shard_map/dot_general | solution.py:70
  526.1 15.0 %fusion.121 = f32[1536,6144]{1,0:T(8,128)} fusion(bf16[128,6144]{1,0:T(8,128)(2,1)S(1)} %copy-done.3, bf16[1,1,128,1536]{3,2,1,0:T(8,128)(2,1)S(1)} %copy-done.7), kind=kOutput, calls=%fused_computation.142 | convolution fusion | flops 2417885184 | bytes 39714816 | tf_op jit(solution)/shard_map/dot_general | solution.py:67
  541.1 5.5 all-gather.39.cloned.1.call-done
  546.6 16.8 %fusion.57 = f32[1536,6144]{1,0:T(8,128)} fusion(bf16[1,1,128,6144]{3,2,1,0:T(8,128)(2,1)} %all-gather.39.cloned.1.call-done, bf16[128,1536]{1,0:T(8,128)(2,1)S(1)} %copy-done.16, bf16[1,1,128,1536]{3,2,1,0:T(8,128)(2,1)S(1)} %copy-done.7), kind=kOutput, calls=%fused_computation.74 | convolution fusion | flops 2420047872 | bytes 40108032 | tf_op jit(solution)/shard_map/dot_general | solution.py:70
  563.4 15.2 %fusion.123 = f32[1536,6144]{1,0:T(8,128)} fusion(bf16[128,6144]{1,0:T(8,128)(2,1)S(1)} %copy-done.4, bf16[1,1,128,1536]{3,2,1,0:T(8,128)(2,1)S(1)} %copy-done.9), kind=kOutput, calls=%fused_computation.143 | convolution fusion | flops 2417885184 | bytes 39714816 | tf_op jit(solution)/shard_map/dot_general | solution.py:67
  578.6 6.1 all-gather.41.cloned.1.call-done
  584.7 16.7 %fusion.55 = f32[1536,6144]{1,0:T(8,128)} fusion(bf16[1,1,128,6144]{3,2,1,0:T(8,128)(2,1)} %all-gather.41.cloned.1.call-done, bf16[128,1536]{1,0:T(8,128)(2,1)S(1)} %copy-done.17, bf16[1,1,128,1536]{3,2,1,0:T(8,128)(2,1)S(1)} %copy-done.9), kind=kOutput, calls=%fused_computation.72 | convolution fusion | flops 2420047872 | bytes 40108032 | tf_op jit(solution)/shard_map/dot_general | solution.py:70
  601.4 14.9 %fusion.125 = f32[1536,6144]{1,0:T(8,128)} fusion(bf16[128,6144]{1,0:T(8,128)(2,1)S(1)} %copy-done.5, bf16[1,1,128,1536]{3,2,1,0:T(8,128)(2,1)S(1)} %copy-done.10), kind=kOutput, calls=%fused_computation.144 | convolution fusion | flops 2417885184 | bytes 39714816 | tf_op jit(solution)/shard_map/dot_general | solution.py:67
  616.3 5.8 all-gather.43.cloned.1.call-done
  622.1 16.9 %fusion.53 = f32[1536,6144]{1,0:T(8,128)} fusion(bf16[1,1,128,6144]{3,2,1,0:T(8,128)(2,1)} %all-gather.43.cloned.1.call-done, bf16[128,1536]{1,0:T(8,128)(2,1)S(1)} %copy-done.18, bf16[1,1,128,1536]{3,2,1,0:T(8,128)(2,1)S(1)} %copy-done.10), kind=kOutput, calls=%fused_computation.70 | convolution fusion | flops 2420047872 | bytes 40108032 | tf_op jit(solution)/shard_map/dot_general | solution.py:70
  639.0 0.9 copy.12
  639.9 19.7 %all-gather.33.cloned.1.call-done = bf16[128,6144]{1,0:T(8,128)(2,1)} async-done(((bf16[128,1536]{1,0:T(8,128)(2,1)}), bf16[128,6144]{1,0:T(8,128)(2,1)}) %all-gather.33.cloned.1.call-update) | async-done | bytes 1572880 | tf_op jit(solution)/shard_map/all_gather | solution.py:49
  659.5 13.2 %fusion.49 = bf16[128,1536]{1,0:T(8,128)(2,1)S(1)} fusion(bf16[128,6144]{1,0:T(8,128)(2,1)} %all-gather.33.cloned.1.call-done, bf16[1,1536,6144]{2,1,0:T(8,128)(2,1)} %param.9), kind=kOutput, calls=%fused_computation.33 | convolution fusion | flops 2416115712 | bytes 20840448 | tf_op jit(solution)/shard_map/dot_general | solution.py:52
  672.7 9.9 %all-gather.13 = bf16[256,1536]{1,0:T(8,128)(2,1)S(1)} all-gather(bf16[128,1536]{1,0:T(8,128)(2,1)S(1)} %fusion.49), channel_id=15, replica_groups=mesh['pipe'=4,'dp'=2,'tensor'=4] {'dp'}, dimensions={0}, use_global_device_ids=true | all-gather | bytes 1179648 | tf_op jit(solution)/shard_map/all_gather | solution.py:55
  682.8 10.7 %fusion.34 = bf16[128,6144]{1,0:T(8,128)(2,1)} fusion(bf16[1,1536,6144]{2,1,0:T(8,128)(2,1)} %param.8, bf16[128,1536]{1,0:T(8,128)(2,1)S(1)} %reduce_sum.64, bf16[1,1,128,1536]{3,2,1,0:T(8,128)(2,1)S(1)} %copy-done.14), kind=kOutput, calls=%fused_computation.28 | convolution fusion | flops 2420834304 | bytes 21233664 | tf_op jit(solution)/shard_map/dot_general | solution.py:62
  693.5 3.9 all-gather.45.cloned.1.call-done
  697.5 33.0 %fusion = bf16[1,1536,6144]{2,1,0:T(8,128)(2,1)} fusion(f32[1536,6144]{1,0:T(8,128)} %fusion.53, f32[1536,6144]{1,0:T(8,128)} %fusion.55, f32[1536,6144]{1,0:T(8,128)} %fusion.57, f32[1536,6144]{1,0:T(8,128)} %fusion.59, pred[]{:T(512)S(6)} %and.20, pred[]{:T(512)S(6)} %and.19, pred[]{:T(512)S(6)} %and.18, pred[]{:T(512)S(6)} %and.17, pred[]{:T(512)S(6)} %and.16, ...), kind=kOutput, calls=%fused_computation.2 | convolution fusion | flops 2514419712 | bytes 172228608 | tf_op jit(solution)/shard_map/dot_general | solution.py:70
  730.4 31.8 %fusion.1 = bf16[1,1536,6144]{2,1,0:T(8,128)(2,1)} fusion(bf16[128,6144]{1,0:T(8,128)(2,1)S(1)} %copy-done.1, f32[1536,6144]{1,0:T(8,128)} %fusion.125, f32[1536,6144]{1,0:T(8,128)} %fusion.123, f32[1536,6144]{1,0:T(8,128)} %fusion.121, f32[1536,6144]{1,0:T(8,128)} %fusion.61, pred[]{:T(512)S(6)} %and.20, pred[]{:T(512)S(6)} %and.19, pred[]{:T(512)S(6)} %and.18, ...), kind=kOutput, calls=%fused_computation.3 | convolution fusion | flops 2512257024 | bytes 171835392 | tf_op jit(solution)/shard_map/dot_general | solution.py:67
  762.3 1.9 fusion.130
  (83 shorter events, 7.5 us)
Async XLA Ops:
  7.2 41.2 %all-gather.35.cloned.1.call-start = ((), (), s32[]{:S(2)}) async-start(), calls=%async_computation.14 | async-start | bytes 1966080 | tf_op jit(solution)/shard_map/all_gather | solution.py:49
  9.0 110.1 %reduce-scatter.6.cloned.1.call-start = ((), (), s32[]{:S(2)}) async-start(), calls=%async_computation.5 | async-start | bytes 1966080 | tf_op jit(solution)/shard_map/reduce_scatter | solution.py:63
  61.6 57.6 %copy-start = (bf16[2,128,1536]{2,1,0:T(8,128)(2,1)S(1)}, bf16[2,128,1536]{2,1,0:T(8,128)(2,1)}, u32[]{:S(2)}) copy-start(bf16[2,128,1536]{2,1,0:T(8,128)(2,1)} %param.5) | copy-start | bytes 2359300
  71.6 59.4 %copy-start.15 = (bf16[128,1536]{1,0:T(8,128)(2,1)}, bf16[128,1536]{1,0:T(8,128)(2,1)S(1)}, u32[]{:S(2)}) copy-start(bf16[128,1536]{1,0:T(8,128)(2,1)S(1)} %reduce_sum.60) | copy-start | bytes 1179652
  82.4 82.3 %all-gather.27.cloned.1.call-start = ((), (), s32[]{:S(2)}) async-start(), calls=%async_computation.6 | async-start | bytes 1966080 | tf_op jit(solution)/shard_map/all_gather | solution.py:49
  120.4 9.8 %collective-permute-start = (bf16[128,1536]{1,0:T(8,128)(2,1)S(1)}, bf16[128,1536]{1,0:T(8,128)(2,1)S(1)}, u32[]{:S(2)}, u32[]{:S(2)}) collective-permute-start(bf16[128,1536]{1,0:T(8,128)(2,1)S(1)} %get-tuple-element.10), channel_id=1, source_target_pairs={{8,0},{16,8},{24,16},{9,1},{17,9},{25,17},{10,2},{18,10},{26,18},{... | collective-permute-start | bytes 1179656 | tf_op jit(solution)/shard_map/ppermute | solution.py:11
  131.0 106.3 %reduce-scatter.8.cloned.1.call-start = ((), (), s32[]{:S(2)}) async-start(), calls=%async_computation.7 | async-start | bytes 1966080 | tf_op jit(solution)/shard_map/reduce_scatter | solution.py:63
  136.4 64.0 %copy-start.6 = (bf16[1,1,128,1536]{3,2,1,0:T(8,128)(2,1)}, bf16[1,1,128,1536]{3,2,1,0:T(8,128)(2,1)S(1)}, u32[]{:S(2)}) copy-start(bf16[1,1,128,1536]{3,2,1,0:T(8,128)(2,1)S(1)} %all-gather.5) | copy-start | bytes 1179652
  178.6 58.6 %copy-start.11 = (bf16[128,1536]{1,0:T(8,128)(2,1)S(1)}, bf16[128,1536]{1,0:T(8,128)(2,1)}, u32[]{:S(2)}) copy-start(bf16[128,1536]{1,0:T(8,128)(2,1)} %bitcast_select_fusion.6) | copy-start | bytes 1179652
  189.7 59.4 %copy-start.20 = (bf16[1,1,64,1536]{3,2,1,0:T(8,128)(2,1)S(1)}, bf16[1,1,64,1536]{3,2,1,0:T(8,128)(2,1)}, u32[]{:S(2)}) copy-start(bf16[1,1,64,1536]{3,2,1,0:T(8,128)(2,1)} %get-tuple-element.17) | copy-start | bytes 589828
  200.5 82.3 %all-gather.29.cloned.1.call-start = ((), (), s32[]{:S(2)}) async-start(), calls=%async_computation.8 | async-start | bytes 1966080 | tf_op jit(solution)/shard_map/all_gather | solution.py:49
  238.5 9.8 %collective-permute-start.1 = (bf16[128,1536]{1,0:T(8,128)(2,1)S(1)}, bf16[128,1536]{1,0:T(8,128)(2,1)S(1)}, u32[]{:S(2)}, u32[]{:S(2)}) collective-permute-start(bf16[128,1536]{1,0:T(8,128)(2,1)S(1)} %get-tuple-element.8), channel_id=1, source_target_pairs={{8,0},{16,8},{24,16},{9,1},{17,9},{25,17},{10,2},{18,10},{26,18},{... | collective-permute-start | bytes 1179656 | tf_op jit(solution)/shard_map/ppermute | solution.py:11
  249.1 106.3 %reduce-scatter.10.cloned.1.call-start = ((), (), s32[]{:S(2)}) async-start(), calls=%async_computation.9 | async-start | bytes 1966080 | tf_op jit(solution)/shard_map/reduce_scatter | solution.py:63
  254.6 64.0 %copy-start.8 = (bf16[1,1,128,1536]{3,2,1,0:T(8,128)(2,1)}, bf16[1,1,128,1536]{3,2,1,0:T(8,128)(2,1)S(1)}, u32[]{:S(2)}) copy-start(bf16[1,1,128,1536]{3,2,1,0:T(8,128)(2,1)S(1)} %all-gather.8) | copy-start | bytes 1179652
  296.8 58.6 %copy-start.12 = (bf16[128,1536]{1,0:T(8,128)(2,1)S(1)}, bf16[128,1536]{1,0:T(8,128)(2,1)}, u32[]{:S(2)}) copy-start(bf16[128,1536]{1,0:T(8,128)(2,1)} %bitcast_select_fusion.5) | copy-start | bytes 1179652
  307.9 59.1 %copy-start.19 = (bf16[1,1,64,1536]{3,2,1,0:T(8,128)(2,1)S(1)}, bf16[1,1,64,1536]{3,2,1,0:T(8,128)(2,1)}, u32[]{:S(2)}) copy-start(bf16[1,1,64,1536]{3,2,1,0:T(8,128)(2,1)} %get-tuple-element.20) | copy-start | bytes 589828
  318.6 82.0 %all-gather.31.cloned.1.call-start = ((), (), s32[]{:S(2)}) async-start(), calls=%async_computation.10 | async-start | bytes 1966080 | tf_op jit(solution)/shard_map/all_gather | solution.py:49
  356.6 9.5 %collective-permute-start.2 = (bf16[128,1536]{1,0:T(8,128)(2,1)S(1)}, bf16[128,1536]{1,0:T(8,128)(2,1)S(1)}, u32[]{:S(2)}, u32[]{:S(2)}) collective-permute-start(bf16[128,1536]{1,0:T(8,128)(2,1)S(1)} %get-tuple-element.6), channel_id=1, source_target_pairs={{8,0},{16,8},{24,16},{9,1},{17,9},{25,17},{10,2},{18,10},{26,18},{... | collective-permute-start | bytes 1179656 | tf_op jit(solution)/shard_map/ppermute | solution.py:11
  366.9 105.4 %reduce-scatter.12.cloned.1.call-start = ((), (), s32[]{:S(2)}) async-start(), calls=%async_computation.11 | async-start | bytes 1966080 | tf_op jit(solution)/shard_map/reduce_scatter | solution.py:63
  424.6 67.4 %copy-start.2 = (bf16[1,128,6144]{2,1,0:T(8,128)(2,1)S(1)}, bf16[1,128,6144]{2,1,0:T(8,128)(2,1)}, u32[]{:S(2)}) copy-start(bf16[1,128,6144]{2,1,0:T(8,128)(2,1)} %all-gather.35.cloned.1.call-done) | copy-start | bytes 4718596
  435.5 73.8 %all-gather.37.cloned.1.call-start = ((), (), s32[]{:S(2)}) async-start(), calls=%async_computation.15 | async-start | bytes 1966080 | tf_op jit(solution)/shard_map/all_gather | solution.py:50
  438.6 108.1 %all-gather.39.cloned.1.call-start = ((), (), s32[]{:S(2)}) async-start(), calls=%async_computation.16 | async-start | bytes 1966080 | tf_op jit(solution)/shard_map/all_gather | solution.py:50
  439.1 145.6 %all-gather.41.cloned.1.call-start = ((), (), s32[]{:S(2)}) async-start(), calls=%async_computation.17 | async-start | bytes 1966080 | tf_op jit(solution)/shard_map/all_gather | solution.py:50
  439.9 182.2 %all-gather.43.cloned.1.call-start = ((), (), s32[]{:S(2)}) async-start(), calls=%async_computation.18 | async-start | bytes 1966080 | tf_op jit(solution)/shard_map/all_gather | solution.py:50
  440.5 219.1 %all-gather.33.cloned.1.call-start = ((), (), s32[]{:S(2)}) async-start(), calls=%async_computation.12 | async-start | bytes 1966080 | tf_op jit(solution)/shard_map/all_gather | solution.py:49
  473.7 9.5 %collective-permute-start.3 = (bf16[128,1536]{1,0:T(8,128)(2,1)S(1)}, bf16[128,1536]{1,0:T(8,128)(2,1)S(1)}, u32[]{:S(2)}, u32[]{:S(2)}) collective-permute-start(bf16[128,1536]{1,0:T(8,128)(2,1)S(1)} %get-tuple-element.4), channel_id=1, source_target_pairs={{8,0},{16,8},{24,16},{9,1},{17,9},{25,17},{10,2},{18,10},{26,18},{... | collective-permute-start | bytes 1179656 | tf_op jit(solution)/shard_map/ppermute | solution.py:11
  484.0 213.4 %all-gather.45.cloned.1.call-start = ((), (), s32[]{:S(2)}) async-start(), calls=%async_computation.19 | async-start | bytes 1966080 | tf_op jit(solution)/shard_map/all_gather | solution.py:50
  484.6 277.7 %reduce-scatter.14.cloned.1.call-start = ((), (), s32[]{:S(2)}) async-start(), calls=%async_computation.13 | async-start | bytes 1966080 | tf_op jit(solution)/shard_map/reduce_scatter | solution.py:63
  506.7 19.4 %copy-start.3 = (bf16[128,6144]{1,0:T(8,128)(2,1)S(1)}, bf16[128,6144]{1,0:T(8,128)(2,1)}, u32[]{:S(2)}) copy-start(bf16[128,6144]{1,0:T(8,128)(2,1)} %all-gather.27.cloned.1.call-done) | copy-start | bytes 4718596
  506.7 19.4 %copy-start.7 = (bf16[1,1,128,1536]{3,2,1,0:T(8,128)(2,1)S(1)}, bf16[1,1,128,1536]{3,2,1,0:T(8,128)(2,1)}, u32[]{:S(2)}) copy-start(bf16[1,1,128,1536]{3,2,1,0:T(8,128)(2,1)} %copy-done.6) | copy-start | bytes 1179652
  526.1 20.5 %copy-start.16 = (bf16[128,1536]{1,0:T(8,128)(2,1)S(1)}, bf16[128,1536]{1,0:T(8,128)(2,1)}, u32[]{:S(2)}) copy-start(bf16[128,1536]{1,0:T(8,128)(2,1)} %reduce_sum.61) | copy-start | bytes 1179652
  541.1 22.3 %copy-start.4 = (bf16[128,6144]{1,0:T(8,128)(2,1)S(1)}, bf16[128,6144]{1,0:T(8,128)(2,1)}, u32[]{:S(2)}) copy-start(bf16[128,6144]{1,0:T(8,128)(2,1)} %all-gather.29.cloned.1.call-done) | copy-start | bytes 4718596
  541.1 22.3 %copy-start.9 = (bf16[1,1,128,1536]{3,2,1,0:T(8,128)(2,1)S(1)}, bf16[1,1,128,1536]{3,2,1,0:T(8,128)(2,1)}, u32[]{:S(2)}) copy-start(bf16[1,1,128,1536]{3,2,1,0:T(8,128)(2,1)} %copy-done.8) | copy-start | bytes 1179652
  563.4 21.3 %copy-start.17 = (bf16[128,1536]{1,0:T(8,128)(2,1)S(1)}, bf16[128,1536]{1,0:T(8,128)(2,1)}, u32[]{:S(2)}) copy-start(bf16[128,1536]{1,0:T(8,128)(2,1)} %reduce_sum.62) | copy-start | bytes 1179652
  578.6 22.8 %copy-start.5 = (bf16[128,6144]{1,0:T(8,128)(2,1)S(1)}, bf16[128,6144]{1,0:T(8,128)(2,1)}, u32[]{:S(2)}) copy-start(bf16[128,6144]{1,0:T(8,128)(2,1)} %all-gather.31.cloned.1.call-done) | copy-start | bytes 4718596
  578.6 22.8 %copy-start.10 = (bf16[1,1,128,1536]{3,2,1,0:T(8,128)(2,1)S(1)}, bf16[1,1,128,1536]{3,2,1,0:T(8,128)(2,1)}, u32[]{:S(2)}) copy-start(bf16[1,1,128,1536]{3,2,1,0:T(8,128)(2,1)} %all-gather.11) | copy-start | bytes 1179652
  601.4 20.7 %copy-start.18 = (bf16[128,1536]{1,0:T(8,128)(2,1)S(1)}, bf16[128,1536]{1,0:T(8,128)(2,1)}, u32[]{:S(2)}) copy-start(bf16[128,1536]{1,0:T(8,128)(2,1)} %reduce_sum.63) | copy-start | bytes 1179652
  639.0 43.8 %copy-start.14 = (bf16[1,1,128,1536]{3,2,1,0:T(8,128)(2,1)S(1)}, bf16[1,1,128,1536]{3,2,1,0:T(8,128)(2,1)}, u32[]{:S(2)}) copy-start(bf16[1,1,128,1536]{3,2,1,0:T(8,128)(2,1)} %all-gather.14) | copy-start | bytes 1179652
  693.5 36.9 %copy-start.1 = (bf16[128,6144]{1,0:T(8,128)(2,1)S(1)}, bf16[128,6144]{1,0:T(8,128)(2,1)}, u32[]{:S(2)}) copy-start(bf16[128,6144]{1,0:T(8,128)(2,1)} %all-gather.33.cloned.1.call-done) | copy-start | bytes 4718596
  730.4 31.8 %copy-start.13 = (bf16[128,1536]{1,0:T(8,128)(2,1)S(1)}, bf16[128,1536]{1,0:T(8,128)(2,1)}, u32[]{:S(2)}) copy-start(bf16[128,1536]{1,0:T(8,128)(2,1)} %bitcast_select_fusion.3) | copy-start | bytes 1179652
Sparse Core Ops, SparseCore 0:
  10.1 38.1 all-gather.34
  82.5 36.6 reduce-scatter.5
  131.1 33.5 all-gather.26
  200.6 36.6 reduce-scatter.7
  249.2 33.5 all-gather.28
  318.7 36.6 reduce-scatter.9
  367.0 33.5 all-gather.30
  435.6 36.6 reduce-scatter.11
  473.9 35.3 all-gather.36
  510.7 35.8 all-gather.38
  548.8 35.8 all-gather.40
  586.1 35.8 all-gather.42
  623.6 35.8 all-gather.32
  661.5 35.8 all-gather.44
  699.6 34.7 reduce-scatter.13
